TPU v7x, 256 devices: a whole 4x4x8 slice. The times are simulated.
256 devices in a mesh: head: 4 (over x_hi, core), seq: 64 (over y, z, x_lo).
Axes of the slice: x: 4 (x_hi: 2, x_lo: 2; x = x_hi * 2 + x_lo), y: 4, z: 8, core: 2. Of those that a mesh axis runs over, the one named last changes fastest.
Arguments:
- queries: bfloat16 [8192, 128, 128], P('seq', 'head'), may hold values from -8 to 8
- keys: bfloat16 [8192, 8, 128], P('seq', 'head'), may hold values from -8 to 8
- values: bfloat16 [8192, 8, 128], P('seq', 'head'), may hold values from -12 to 12
- feat_q: float32 [128, 128, 64], P('head'), may hold values from -0.5 to 0.5
- key_feature_weights: float32 [8, 128, 64], P('head'), may hold values from -0.5 to 0.5
- doc_start: int32 [8192], P('seq'), may hold values from 0 to 8191, as said below
Outputs:
- teacher_out: bfloat16 [8192, 128, 128], P('seq', 'head')
- student_out: float32 [8192, 128, 128], P('seq', 'head')
- grad_wq: float32 [128, 128, 64], P('head')
- grad_wk: float32 [8, 128, 64], P('head')
Inputs may be any that keep to these rules, and one draw needn't show every extreme that they name: doc_start never falls along the sequence, doc_start[t] <= t, doc_start[0] = 0, and all tokens of one document share it; the sequence holds at most 4 documents.
All inputs are finite; a program needn't handle non-finite values.
Results may differ from a plain program's by a relative error of at most 0.0034.
Values may be sent and summed in bfloat16 or wider, within the bound.
A program may use at most 128 MiB of HBM per device.

v0:
```python
import functools, math
import jax, jax.numpy as jnp
from jax import lax
from jax.experimental import pallas as pl
from jax.experimental.pallas import tpu as pltpu
from jax.sharding import PartitionSpec as P

F32, BF16 = jnp.float32, jnp.bfloat16
NN = (((1,), (0,)), ((), ()))
NT = (((1,), (1,)), ((), ()))
TN = (((0,), (0,)), ((), ()))
LOW = -1e30
BATCH = 8
SPAN, TILE = 1024, 128
PASS = (3, 3, 3, 3, 2, 3, 3, 2, 2)


def dot(a, b, dims=NN):
    return lax.dot_general(a, b, dims, preferred_element_type=F32)


def halves(x):
    hi = x.astype(BF16)
    return hi, (x - hi.astype(F32)).astype(BF16)


def soft(x):
    e = jnp.exp(-jnp.abs(x))
    one = 1.0 + e
    log = jnp.where(e < 1e-3, e * (1.0 - e * (0.5 - e * (1.0 / 3.0))), jnp.log(one))
    return e, log, 1.0 / one


def soft_lanes(x):
    e, log, inverse = soft(x)
    return jnp.maximum(x, 0.0) + log, jnp.where(x >= 0.0, 1.0, e) * inverse


def soft_rows(x):
    e, log, inverse = soft(x)
    other = e * inverse
    feat = jnp.concatenate([jnp.maximum(x, 0.0) + log, jnp.maximum(-x, 0.0) + log], axis=0)
    slope = jnp.concatenate(
        [jnp.where(x >= 0.0, inverse, other), jnp.where(x >= 0.0, other, inverse)], axis=0
    )
    return feat, slope


def stacked(a, b):
    both = dot(jnp.concatenate(a, axis=0), b)
    return both[: both.shape[0] // 2] + both[both.shape[0] // 2 :]


def dots(passes, a, b, dims=NN):
    out = dot(a[0], b[0], dims)
    if passes > 1:
        out = out + dot(a[1], b[0], dims)
    if passes > 2:
        out = out + dot(a[0], b[1], dims)
    return out


def signed(weight):
    return jnp.concatenate([weight, -weight], axis=0)


def compute(span, tile, tokens, pos, doc_ref, k_ref, v_ref, q_ref, wq_ref, wk_ref,
            t_ref, s_ref, g_ref,
            top, acc, sig, state, dstate, dkey, wide, q_s):
    slots = span // 128
    heads = q_ref.shape[1]
    mine, first = lax.axis_index("seq"), pos[0]
    begin = mine * 128
    first_slot = first // 128
    blocks = (mine - first_slot + slots - 1) // slots
    logit = math.log2(math.e) / math.sqrt(128)
    lanes = lax.broadcasted_iota(jnp.int32, (1, span), 1)
    ones = jnp.ones((span, 128), BF16)

    def loads(i):
        at = jnp.minimum(first_slot + i * slots, 64 - slots)
        k = k_ref[pl.ds(at, slots), 0].reshape(span, 128)
        v = v_ref[pl.ds(at, slots), 0].reshape(span, 128)
        key = at * 128 + lanes
        live = (key >= jnp.maximum(first, (first_slot + i * slots) * 128)) & (key < begin)
        return k, jnp.concatenate([v, ones], axis=1), live

    top[...] = jnp.full_like(top, LOW)
    acc[...] = jnp.zeros_like(acc)
    state[...] = jnp.zeros_like(state)
    dstate[...] = jnp.zeros_like(dstate)
    dkey[...] = jnp.zeros_like(dkey)
    wkt = jnp.concatenate(halves(wk_ref[0]), axis=1)
    wide[...] = q_ref[...].astype(F32)
    for h in range(heads):
        q_s[h] = wide[:, h, :].astype(BF16)

    def softmax_step(rows, raw, bias, v2):
        if bias is not None:
            raw = raw + bias
        old = top[rows, :]
        new = jnp.maximum(old, jnp.max(raw, axis=1, keepdims=True))
        base = new * logit
        weight = jnp.exp2(raw * logit - base[:, :1]).astype(BF16)
        shrink = jnp.exp2(old * logit - base)
        top[rows, :] = new
        acc[rows, :] = acc[rows, :] * jnp.concatenate([shrink, shrink], axis=1) + dot(weight, v2)

    def scores(r, k):
        q = q_s[r * (tile // 128) : (r + 1) * (tile // 128)].reshape(tile, 128)
        return dot(q, k, NT)

    def attend(k, v2, bias):
        count = heads * 128 // tile
        ahead = scores(0, k)
        for r in range(count):
            raw = ahead
            if r + 1 < count:
                ahead = scores(r + 1, k)
            softmax_step(slice(r * tile, (r + 1) * tile), raw, bias, v2)

    def prefix(i, _):
        k, v2, live = loads(i)
        feat, slope = soft_rows(dot(wkt, jnp.concatenate([k, k], axis=1), NT))
        feat = jnp.where(live, feat, 0.0)
        sig[i] = jnp.where(live, slope, 0.0)
        state[...] += stacked(halves(feat), v2)
        edge = (i == 0) | (i == blocks - 1)

        @pl.when(edge)
        def _():
            attend(k, v2, jnp.where(live, 0.0, LOW))

        @pl.when(jnp.logical_not(edge))
        def _():
            attend(k, v2, None)

        return 0

    lax.fori_loop(0, blocks, prefix, 0)

    doc = jnp.broadcast_to(doc_ref[...], (128, 128)).T
    at_s = lax.broadcasted_iota(jnp.int32, (128, 128), 1)
    at_t = lax.broadcasted_iota(jnp.int32, (128, 128), 0)
    allowed = (at_s <= at_t) & (at_s + begin >= doc)

    def spread(x):
        return jnp.concatenate([x] * BATCH, axis=0)

    match = spread((doc == first).astype(F32))
    match2 = jnp.concatenate([match, match], axis=1)
    bias = spread(jnp.where(allowed, 0.0, LOW))
    keep = spread(jnp.where(allowed, 1.0, 0.0))
    k = k_ref[mine, 0]
    v2 = jnp.concatenate([v_ref[mine, 0], ones[:128]], axis=1)
    kk = jnp.concatenate([k, k], axis=1)
    kf = halves(soft_lanes(dot(kk, signed(wkt), NT))[0])
    sh, sl = halves(state[...])
    bh = jnp.concatenate([v2, sh], axis=0)
    bl = jnp.concatenate([jnp.zeros_like(v2), sl], axis=0)
    full = BATCH * 128

    def some(b, _):
        h0 = b * BATCH
        rows = pl.ds(pl.multiple_of(b * full, full), full)
        q = q_s[pl.ds(h0, BATCH)].reshape(full, 128)
        top[rows, :] = jnp.where(match > 0.0, top[rows, :], LOW)
        acc[rows, :] = acc[rows, :] * match2
        softmax_step(rows, dot(q, k, NT), bias, v2)
        total = acc[rows, :]
        teacher = (total[:, :128] / total[:, 128:]).astype(BF16)
        for j in range(BATCH):
            wide[:, h0 + j, :] = teacher[j * 128 : (j + 1) * 128].astype(F32)
        both = []
        for j in range(BATCH):
            wq2 = signed(jnp.concatenate(halves(wq_ref[h0 + j]), axis=1))
            qj = q_s[h0 + j]
            both.append(dot(jnp.concatenate([qj, qj], axis=1), wq2, NT))
        feat, slope = soft_lanes(jnp.concatenate(both, axis=0))
        fs = halves(feat)
        sim = dots(PASS[0], fs, kf, NT) * keep
        a = halves(jnp.concatenate([sim, feat * match], axis=1))
        out = dots(PASS[1], a, (bh, bl))
        inverse = 1.0 / out[:, 128:]
        student = out[:, :128] * inverse
        for j in range(BATCH):
            s_ref[:, h0 + j, :] = student[j * 128 : (j + 1) * 128]
        tangent = (student - teacher.astype(F32)) * (inverse * (1.0 / math.sqrt(tokens)))
        loss = -jnp.sum(tangent * student, axis=1, keepdims=True) * (1.0 / 128.0)
        d = jnp.concatenate([tangent, jnp.broadcast_to(loss, (full, 128))], axis=1)
        da = dots(PASS[2], halves(d), (bh, bl), NT)
        dsim = halves(da[:, :128] * keep)
        dfeat = dots(PASS[3], dsim, kf) + da[:, 128:] * match
        dp = halves(dfeat * slope)
        for j in range(BATCH):
            part = slice(j * 128, (j + 1) * 128)
            gt = dots(PASS[4], (dp[0][part], dp[1][part]), (q_s[h0 + j],), TN)
            g_ref[h0 + j, 0:64] = gt[:64] - gt[64:]
        dkey[...] += dots(PASS[5], fs, dsim, TN)
        dstate[...] += dots(PASS[6], fs, halves(d * match2), TN)
        return 0

    for b in range(heads // BATCH):
        some(b, 0)
    t_ref[...] = wide[...].astype(BF16)

    _, slope = soft_rows(dot(wkt, kk, NT))
    state[:, :128] = stacked(halves(dkey[...] * slope), k)
    ds = jnp.concatenate(halves(dstate[...]), axis=0)

    def pull(i, _):
        k, v2, _ = loads(i)
        dk = dot(ds, v2, NT)
        state[:, :128] += stacked(halves((dk[:128] + dk[128:]) * sig[i]), k)
        return 0

    lax.fori_loop(0, blocks, pull, 0)
    gk = state[:64, :128] - state[64:, :128]
    pad = jnp.zeros((4, 128), F32)
    for j in range(heads):
        g_ref[j, 64:72] = jnp.concatenate([gk[4 * j : 4 * j + 4], pad], axis=0)


def run(doc, kv, q, wq, wk, tokens, span, tile):
    groups = wk.shape[0]
    heads = q.shape[1] // groups
    spec = pl.BlockSpec
    return pl.pallas_call(
        functools.partial(compute, span, tile, tokens),
        out_shape=(
            jax.ShapeDtypeStruct(q.shape, BF16),
            jax.ShapeDtypeStruct(q.shape, F32),
            jax.ShapeDtypeStruct((q.shape[1], 72, 128), F32),
        ),
        grid=(groups,),
        in_specs=[
            spec(memory_space=pltpu.SMEM),
            spec((1, 128), lambda g: (0, 0)),
            spec((64, 1, 128, 128), lambda g: (0, g, 0, 0)),
            spec((64, 1, 128, 128), lambda g: (0, g + groups, 0, 0)),
            spec((128, heads, 128), lambda g: (0, g, 0)),
            spec((heads, 64, 128), lambda g: (g, 0, 0)),
            spec((1, 64, 128), lambda g: (g, 0, 0)),
        ],
        out_specs=(
            spec((128, heads, 128), lambda g: (0, g, 0)),
            spec((128, heads, 128), lambda g: (0, g, 0)),
            spec((heads, 72, 128), lambda g: (g, 0, 0)),
        ),
        scratch_shapes=[
            pltpu.VMEM((heads * 128, 128), F32),
            pltpu.VMEM((heads * 128, 256), F32),
            pltpu.VMEM((64 * 128 // span, 128, span), F32),
            pltpu.VMEM((128, 256), F32),
            pltpu.VMEM((128, 256), F32),
            pltpu.VMEM((128, 128), F32),
            pltpu.VMEM((128, heads, 128), F32),
            pltpu.VMEM((heads, 128, 128), BF16),
        ],
        compiler_params=pltpu.CompilerParams(
            dimension_semantics=("arbitrary",), vmem_limit_bytes=58 * 2**20
        ),
    )(doc, doc.reshape(1, 128), kv, kv, q, wq, wk)


MESH = pl.DeviceIdType.MESH


def place():
    at = lax.axis_index("seq")
    return at // 16, (at // 2) % 8, at % 2


def seq_of(y, z, x):
    return {"seq": ((y + 4) % 4 * 8 + (z + 8) % 8) * 2 + x}


def greet(peers):
    barrier = pltpu.get_barrier_semaphore()
    for peer in peers:
        pl.semaphore_signal(barrier, inc=1, device_id=peer, device_id_type=MESH)
    pl.semaphore_wait(barrier, len(peers))


class Copies:
    def __init__(self, out_sem, in_sem):
        self.sems, self.all = (out_sem, in_sem), []

    def __call__(self, src, dst, peer):
        n = len(self.all)
        copy = pltpu.make_async_remote_copy(
            src_ref=src,
            dst_ref=dst,
            send_sem=self.sems[0].at[n],
            recv_sem=self.sems[1].at[n],
            device_id=peer,
            device_id_type=MESH,
        )
        copy.start()
        self.all.append(copy)
        return copy

    def finish(self):
        for copy in self.all:
            copy.wait_send()


PART_A, PART_B, PART_C = (0, 96, 176), (176, 272, 352), (352, 432, 512)


def gather_kernel(own, out, out_sem, in_sem, own_sem):
    y, z, x = place()
    greet(
        [seq_of(y, z, 1 - x)]
        + [seq_of(y + k, z, x) for k in (1, -1)]
        + [seq_of(y, z + k, x) for k in (1, -1)]
    )
    send = Copies(out_sem, in_sem)

    def ring(part, region, axis, source=None):
        size = 8 if axis == "z" else 4
        here = z if axis == "z" else y

        def toward(k):
            return seq_of(y, z + k, x) if axis == "z" else seq_of(y + k, z, x)

        def rows(a, b):
            return pl.ds(part[a], part[b] - part[a])

        for step in range(1, size // 2 + 1):
            last = step == size // 2
            cuts = ((0, 1), (1, 2)) if last else ((0, 2), (0, 2))
            back, fore = (here + size - step + 1) % size, (here + step - 1) % size
            pair = []
            for at, cut, k in ((back, cuts[0], 1), (fore, cuts[1], -1)):
                target = region(at, rows(*cut))
                from_here = source(rows(*cut)) if source is not None and step == 1 else target
                pair.append(send(from_here, target, toward(k)))
            yield
            for copy in pair:
                copy.wait_recv()

    keep = pltpu.make_async_copy(own, out.at[y, z, x], own_sem)
    keep.start()
    rows_c = pl.ds(PART_C[0], PART_C[2] - PART_C[0])
    across = seq_of(y, z, 1 - x)
    first = pl.ds(0, PART_C[0])
    cross = send(own.at[first], out.at[y, z, x, first], across)
    cz = ring(PART_C, lambda i, r: out.at[y, i, x, r], "z", lambda r: own.at[r])
    ay = ring(PART_A, lambda i, r: out.at[i, z, :, r], "y")
    bz = ring(PART_B, lambda i, r: out.at[y, i, :, r], "z")
    az = ring(PART_A, lambda i, r: out.at[:, i, :, r], "z")
    cy = ring(PART_C, lambda i, r: out.at[i, :, x, r], "y")
    by = ring(PART_B, lambda i, r: out.at[i, :, :, r], "y")
    waits = [cross]

    def over(i):
        region = out.at[i, :, x, rows_c]
        waits.append(send(region, region, across))

    def go(stream):
        next(stream, None)

    go(cz)
    keep.wait()
    cross.wait_recv()
    waits.clear()
    go(ay)
    go(bz)
    go(cz)
    go(ay)
    go(bz)
    go(cz)
    go(ay)
    go(az)
    go(bz)
    go(cz)
    go(cz)
    go(cy)
    over(y)
    go(bz)
    go(az)
    go(bz)
    go(by)
    go(cy)
    over((y + 3) % 4)
    over((y + 1) % 4)
    go(az)
    go(cy)
    over((y + 2) % 4)
    go(by)
    go(az)
    go(by)
    go(az)
    for copy in waits:
        copy.wait_recv()
    send.finish()


def gather(own):
    return pl.pallas_call(
        gather_kernel,
        out_shape=jax.ShapeDtypeStruct((4, 8, 2) + own.shape, own.dtype),
        in_specs=[pl.BlockSpec(memory_space=pltpu.VMEM)],
        out_specs=pl.BlockSpec(memory_space=pl.ANY),
        scratch_shapes=[
            pltpu.SemaphoreType.DMA((48,)),
            pltpu.SemaphoreType.DMA((48,)),
            pltpu.SemaphoreType.DMA,
        ],
        compiler_params=pltpu.CompilerParams(collective_id=0, has_side_effects=True),
    )(own)


def reduce_kernel(entries, g, out_q, out_k, far, near, acc, mid, zin, piece, xin, sq, sqin, full, out_sem, in_sem):
    y, z, x = place()
    head = lax.axis_index("head")
    peers_z = [seq_of(y, z + k, x) for k in range(1, 8)]
    peers_h = [{"head": (head + k) % 4} for k in range(1, 4)]
    up, down, across = seq_of(y + 1, z, x), seq_of(y - 1, z, x), seq_of(y, z, 1 - x)
    greet([up, down, across] + peers_z + peers_h)
    send = Copies(out_sem, in_sem)
    lo, hi = pl.ds(0, 4), pl.ds(4, 4)
    opposite, above, below = (y + 2) % 4, (y + 1) % 4, (y + 3) % 4
    far_up = send(g.at[opposite, lo], far.at[0], up)
    far_down = send(g.at[opposite, hi], far.at[1], down)
    near_up = send(g.at[above, hi], near.at[0], up)
    near_down = send(g.at[below, lo], near.at[1], down)
    far_up.wait_recv()
    acc[0] = g[above, lo] + far[0]
    acc_up = send(acc.at[0], near.at[2], up)
    far_down.wait_recv()
    acc[1] = g[below, hi] + far[1]
    acc_down = send(acc.at[1], near.at[3], down)
    near_up.wait_recv()
    near_down.wait_recv()
    acc_up.wait_recv()
    acc_down.wait_recv()
    mid[lo] = g[y, lo] + near[1] + near[2]
    mid[hi] = g[y, hi] + near[0] + near[3]
    parts = [send(mid.at[(z + k) % 8], zin.at[k - 1], peers_z[k - 1]) for k in range(1, 8)]
    total = mid[z]
    for k, part in enumerate(parts):
        part.wait_recv()
        total = total + zin[k]
    piece[...] = total
    swap = send(piece, xin, across)
    swap.wait_recv()
    total = total + xin[...]
    squares = total[0:8] * total[0:8]
    for k in range(1, 9):
        squares = squares + total[8 * k : 8 * k + 8] * total[8 * k : 8 * k + 8]
    sq[...] = squares
    shares = [send(sq, sqin.at[k - 1], peers_h[k - 1]) for k in range(1, 4)]
    full[y, z, 0:64] = total[0:64].astype(jnp.bfloat16)
    for k, share in enumerate(shares):
        share.wait_recv()
        squares = squares + sqin[k]
    squares = jnp.sum(squares, axis=0, keepdims=True)
    coarse = squares.astype(jnp.bfloat16).astype(jnp.float32)
    row = lax.broadcasted_iota(jnp.int32, (8, 128), 0)
    pair = jnp.where(row == 0, coarse, jnp.where(row == 1, squares - coarse, 0.0))
    full[y, z, 64:80] = jnp.concatenate([total[64:72], pair], axis=0).astype(jnp.bfloat16)
    shard = full.at[y, z]
    for part in [send(shard, shard, peer) for peer in peers_z]:
        part.wait_recv()
    slab = full.at[y]
    both = [send(slab, slab, up), send(slab, slab, down)]
    both[0].wait_recv()
    half = full.at[below, lo]
    last = [send(half, half, up)]
    both[1].wait_recv()
    half = full.at[above, hi]
    last.append(send(half, half, down))
    for copy in last:
        copy.wait_recv()
    ends = [full[k // 8, k % 8, 64:80].astype(jnp.float32) for k in range(32)]
    squares = ends[0][8:16]
    for end in ends[1:]:
        squares = squares + end[8:16]
    factor = 1.0 / jnp.sqrt(jnp.broadcast_to(jnp.sum(squares) * (1.0 / entries) + 1e-6, (64, 128)))
    for k, end in enumerate(ends):
        out_k[k // 16, 4 * (k % 16) : 4 * (k % 16) + 4] = end[0:4] * factor[0:4]

    def scale(k, _):
        out_q[k] = full[k // 8, k % 8, 0:64].astype(jnp.float32) * factor
        return 0

    lax.fori_loop(0, 32, scale, 0)
    send.finish()


def reduce(g, entries):
    f32 = jnp.float32
    return pl.pallas_call(
        functools.partial(reduce_kernel, entries),
        out_shape=(
            jax.ShapeDtypeStruct((32, 64, 128), f32),
            jax.ShapeDtypeStruct((2, 64, 128), f32),
        ),
        in_specs=[pl.BlockSpec(memory_space=pltpu.VMEM)],
        out_specs=(pl.BlockSpec(memory_space=pltpu.VMEM),) * 2,
        scratch_shapes=[
            pltpu.VMEM((2, 4, 72, 128), f32),
            pltpu.VMEM((4, 4, 72, 128), f32),
            pltpu.VMEM((2, 4, 72, 128), f32),
            pltpu.VMEM((8, 72, 128), f32),
            pltpu.VMEM((7, 72, 128), f32),
            pltpu.VMEM((72, 128), f32),
            pltpu.VMEM((72, 128), f32),
            pltpu.VMEM((8, 128), f32),
            pltpu.VMEM((3, 8, 128), f32),
            pltpu.VMEM((4, 8, 80, 128), jnp.bfloat16),
            pltpu.SemaphoreType.DMA((32,)),
            pltpu.SemaphoreType.DMA((32,)),
        ],
        compiler_params=pltpu.CompilerParams(collective_id=1, has_side_effects=True),
    )(g)


def shards(queries, keys, values, feat_q, key_feature_weights, doc_start):
    rows, heads, width = queries.shape
    groups = keys.shape[1]
    tokens = rows * lax.axis_size("seq")
    kv = jnp.concatenate([keys, values], axis=1).transpose(1, 0, 2).reshape(2 * groups * rows, width)
    gathered = gather(kv).reshape(64, 2 * groups, rows, width)
    teacher, student, g = run(
        doc_start,
        gathered,
        queries,
        feat_q.transpose(0, 2, 1),
        key_feature_weights.transpose(0, 2, 1),
        tokens,
        SPAN,
        TILE,
    )
    entries = (heads + groups) * lax.axis_size("head") * width * 64
    gq, gk = reduce(g.reshape(4, 8, 72, 128), entries)
    return teacher, student, gq.transpose(0, 2, 1), gk.transpose(0, 2, 1)


def solution(mesh):
    placed = (
        P("seq", "head", None),
        P("seq", "head", None),
        P("seq", "head", None),
        P("head", None, None),
        P("head", None, None),
        P("seq"),
    )
    return jax.shard_map(
        shards,
        mesh=mesh,
        in_specs=placed,
        out_specs=placed[:2] + placed[3:5],
        check_vma=False,
    )
```

profile of v0, /device:TPU:8, one launch (start us, length us, event | category | flops | bytes accessed | tf_op | source)
XLA Modules:
  0.0 175.9 jit_solution(7583126923821722210)
XLA Ops:
  0.6 1.0 maximum_bitcast_fusion
  1.6 0.7 copy.10
  2.3 66.7 %shard_map.93 = bf16[4,8,2,512,128]{4,3,2,1,0:T(8,128)(2,1)} custom-call(bf16[512,128]{1,0:T(8,128)(2,1)} %bitcast.15), custom_call_target="tpu_custom_call" | custom-call | tf_op jit(solution)/shard_map/pallas_call | solution.py:401
  69.1 41.1 %shard_map.94 = (bf16[128,32,128]{2,1,0:T(8,128)(2,1)}, f32[128,32,128]{2,1,0:T(8,128)}, f32[32,72,128]{2,1,0:T(8,128)}) custom-call(s32[128]{0:T(128)} %pos.1, s32[1,128]{1,0:T(1,128)} %bitcast.18, bf16[64,4,128,128]{3,2,1,0:T(8,128)(2,1)} %bitcast.10, bf16[64,4,128,128]{3,2,1,0:T(8,128)(2,1)} %bitcast.11, bf16[128,32,128]{2,1,0:T(8,128)(2,1)} %q_ref.1, ...), custom_call_target="tpu_custom_call" | custom-call | tf_op jit(solution)/shard_map/pallas_call | solution.py:228
  110.2 62.7 %shard_map.95 = (f32[32,64,128]{2,1,0:T(8,128)}, f32[2,64,128]{2,1,0:T(8,128)}) custom-call(f32[4,8,72,128]{3,2,1,0:T(8,128)} %bitcast.12), custom_call_target="tpu_custom_call" | custom-call | tf_op jit(solution)/shard_map/pallas_call | solution.py:495
  172.9 0.0 copy-start
  172.9 2.3 %copy.13 = f32[32,128,64]{1,2,0:T(8,128)} copy(f32[32,128,64]{1,2,0:T(8,128)} %bitcast.14) | data formatting | bytes 2097152
  175.2 0.0 copy-done
  175.2 0.6 copy.14
Async XLA Ops:
  172.9 2.4 %copy-start = (f32[2,64,128]{2,1,0:T(8,128)S(1)}, f32[2,64,128]{2,1,0:T(8,128)}, u32[]{:S(2)}) copy-start(f32[2,64,128]{2,1,0:T(8,128)} %get-tuple-element.13) | copy-start | bytes 196612
where the time goes:
time: 177 us; the launch traced here: 176 us
  Pallas kernels  171 us (97%)
  local copies, waits for them, and re-layouts  3.65 us (2%)
    pallas_call x1, Pallas kernels, gather(): pl.pallas_call(gather_kernel, out_shape=jax.ShapeDtypeStruct((4, 8, 2) +...  66.7 us
    pallas_call x1, Pallas kernels, reduce(): pl.pallas_call(functools.partial(reduce_kernel, entries), out_shape=(jax....  62.7 us
    pallas_call x1, Pallas kernels, run(): pl.pallas_call(functools.partial(compute, span, tile, tokens), out_shape=...  41.1 us

commit v1 on v0

--- a/solution.py
+++ b/solution.py
@@ -10,7 +10,7 @@
 NT = (((1,), (1,)), ((), ()))
 TN = (((0,), (0,)), ((), ()))
 LOW = -1e30
-BATCH = 8
+BATCH = 16
 SPAN, TILE = 1024, 128
 PASS = (3, 3, 3, 3, 2, 3, 3, 2, 2)
 
@@ -305,7 +305,7 @@
             copy.wait_send()
 
 
-PART_A, PART_B, PART_C = (0, 96, 176), (176, 272, 352), (352, 432, 512)
+PART_A, PART_B, PART_C = (0, 96, 176), (176, 256, 320), (320, 416, 512)
 
 
 def gather_kernel(own, out, out_sem, in_sem, own_sem):
@@ -345,53 +345,35 @@
     rows_c = pl.ds(PART_C[0], PART_C[2] - PART_C[0])
     across = seq_of(y, z, 1 - x)
     first = pl.ds(0, PART_C[0])
-    cross = send(own.at[first], out.at[y, z, x, first], across)
     cz = ring(PART_C, lambda i, r: out.at[y, i, x, r], "z", lambda r: own.at[r])
     ay = ring(PART_A, lambda i, r: out.at[i, z, :, r], "y")
     bz = ring(PART_B, lambda i, r: out.at[y, i, :, r], "z")
     az = ring(PART_A, lambda i, r: out.at[:, i, :, r], "z")
     cy = ring(PART_C, lambda i, r: out.at[i, :, x, r], "y")
     by = ring(PART_B, lambda i, r: out.at[i, :, :, r], "y")
-    waits = [cross]
+    waits = []
 
     def over(i):
         region = out.at[i, :, x, rows_c]
         waits.append(send(region, region, across))
 
-    def go(stream):
-        next(stream, None)
+    def go(*streams):
+        for stream in streams:
+            next(stream, None)
 
     go(cz)
+    cross = send(own.at[first], out.at[y, z, x, first], across)
     keep.wait()
+    go(cz)
     cross.wait_recv()
-    waits.clear()
-    go(ay)
-    go(bz)
-    go(cz)
-    go(ay)
-    go(bz)
-    go(cz)
-    go(ay)
-    go(az)
-    go(bz)
-    go(cz)
-    go(cz)
-    go(cy)
+    go(ay, bz, cz, ay, cz, ay, bz, cz, cy)
     over(y)
-    go(bz)
-    go(az)
-    go(bz)
-    go(by)
-    go(cy)
+    go(az, bz, cy)
     over((y + 3) % 4)
     over((y + 1) % 4)
-    go(az)
-    go(cy)
+    go(bz, az, bz, by, az, cy)
     over((y + 2) % 4)
-    go(by)
-    go(az)
-    go(by)
-    go(az)
+    go(by, az, by, az)
     for copy in waits:
         copy.wait_recv()
     send.finish()

time: 177 us -> 178 us (level)
  Pallas kernels: 171 us -> 173 us
    pallas_call x1, Pallas kernels: 62.7 us -> 72.1 us  [reduce(): pl.pallas_call(functools.partial(reduce_kernel, entries), out_shape=(jax....]
    pallas_call x1, Pallas kernels: 66.7 us -> 60.7 us  [gather(): pl.pallas_call(gather_kernel, out_shape=jax.ShapeDtypeStruct((4, 8, 2) +...]
where the time goes in v1:
time: 178 us
  Pallas kernels  173 us (97%)
  local copies, waits for them, and re-layouts  3.65 us (2%)
    pallas_call x1, Pallas kernels, reduce(): pl.pallas_call(functools.partial(reduce_kernel, entries), out_shape=(jax....  72.1 us
    pallas_call x1, Pallas kernels, gather(): pl.pallas_call(gather_kernel, out_shape=jax.ShapeDtypeStruct((4, 8, 2) +...  60.7 us
    pallas_call x1, Pallas kernels, run(): pl.pallas_call(functools.partial(compute, span, tile, tokens), out_shape=...  39.7 us

profile of v1, /device:TPU:8, one launch (start us, length us, event | category | flops | bytes accessed | tf_op | source)
XLA Modules:
  0.0 177.8 jit_solution(10891210631515249336)
XLA Ops:
  0.6 1.0 maximum_bitcast_fusion
  1.6 0.7 copy.10
  2.3 60.7 %shard_map.93 = bf16[4,8,2,512,128]{4,3,2,1,0:T(8,128)(2,1)} custom-call(bf16[512,128]{1,0:T(8,128)(2,1)} %bitcast.15), custom_call_target="tpu_custom_call" | custom-call | tf_op jit(solution)/shard_map/pallas_call | solution.py:383
  63.1 39.7 %shard_map.94 = (bf16[128,32,128]{2,1,0:T(8,128)(2,1)}, f32[128,32,128]{2,1,0:T(8,128)}, f32[32,72,128]{2,1,0:T(8,128)}) custom-call(s32[128]{0:T(128)} %pos.1, s32[1,128]{1,0:T(1,128)} %bitcast.18, bf16[64,4,128,128]{3,2,1,0:T(8,128)(2,1)} %bitcast.10, bf16[64,4,128,128]{3,2,1,0:T(8,128)(2,1)} %bitcast.11, bf16[128,32,128]{2,1,0:T(8,128)(2,1)} %q_ref.1, ...), custom_call_target="tpu_custom_call" | custom-call | tf_op jit(solution)/shard_map/pallas_call | solution.py:228
  102.8 72.1 %shard_map.95 = (f32[32,64,128]{2,1,0:T(8,128)}, f32[2,64,128]{2,1,0:T(8,128)}) custom-call(f32[4,8,72,128]{3,2,1,0:T(8,128)} %bitcast.12), custom_call_target="tpu_custom_call" | custom-call | tf_op jit(solution)/shard_map/pallas_call | solution.py:477
  174.9 0.0 copy-start
  174.9 2.3 %copy.13 = f32[32,128,64]{1,2,0:T(8,128)} copy(f32[32,128,64]{1,2,0:T(8,128)} %bitcast.14) | data formatting | bytes 2097152
  177.2 0.0 copy-done
  177.2 0.6 copy.14
Async XLA Ops:
  174.9 2.4 %copy-start = (f32[2,64,128]{2,1,0:T(8,128)S(1)}, f32[2,64,128]{2,1,0:T(8,128)}, u32[]{:S(2)}) copy-start(f32[2,64,128]{2,1,0:T(8,128)} %get-tuple-element.13) | copy-start | bytes 196612

commit v2 on v1

--- a/solution.py
+++ b/solution.py
@@ -72,18 +72,20 @@
     mine, first = lax.axis_index("seq"), pos[0]
     begin = mine * 128
     first_slot = first // 128
-    blocks = (mine - first_slot + slots - 1) // slots
+    whole = (mine - first_slot) // slots
+    rest = (mine - first_slot) % slots
+    blocks = whole + jnp.where(rest > slots // 2, 1, 0)
+    short = (rest > 0) & (rest <= slots // 2)
     logit = math.log2(math.e) / math.sqrt(128)
-    lanes = lax.broadcasted_iota(jnp.int32, (1, span), 1)
     ones = jnp.ones((span, 128), BF16)
 
-    def loads(i):
-        at = jnp.minimum(first_slot + i * slots, 64 - slots)
-        k = k_ref[pl.ds(at, slots), 0].reshape(span, 128)
-        v = v_ref[pl.ds(at, slots), 0].reshape(span, 128)
-        key = at * 128 + lanes
+    def loads(i, size):
+        at = jnp.minimum(first_slot + i * slots, 64 - size)
+        k = k_ref[pl.ds(at, size), 0].reshape(size * 128, 128)
+        v = v_ref[pl.ds(at, size), 0].reshape(size * 128, 128)
+        key = at * 128 + lax.broadcasted_iota(jnp.int32, (1, size * 128), 1)
         live = (key >= jnp.maximum(first, (first_slot + i * slots) * 128)) & (key < begin)
-        return k, jnp.concatenate([v, ones], axis=1), live
+        return k, jnp.concatenate([v, ones[: size * 128]], axis=1), live
 
     top[...] = jnp.full_like(top, LOW)
     acc[...] = jnp.zeros_like(acc)
@@ -119,17 +121,21 @@
                 ahead = scores(r + 1, k)
             softmax_step(slice(r * tile, (r + 1) * tile), raw, bias, v2)
 
-    def prefix(i, _):
-        k, v2, live = loads(i)
+    def learn(i, size):
+        k, v2, live = loads(i, size)
         feat, slope = soft_rows(dot(wkt, jnp.concatenate([k, k], axis=1), NT))
         feat = jnp.where(live, feat, 0.0)
-        sig[i] = jnp.where(live, slope, 0.0)
+        sig[i, :, : size * 128] = jnp.where(live, slope, 0.0)
         state[...] += stacked(halves(feat), v2)
-        edge = (i == 0) | (i == blocks - 1)
+        return k, v2, jnp.where(live, 0.0, LOW)
+
+    def prefix(i, _):
+        k, v2, bias = learn(i, slots)
+        edge = (i == 0) | (i == whole)
 
         @pl.when(edge)
         def _():
-            attend(k, v2, jnp.where(live, 0.0, LOW))
+            attend(k, v2, bias)
 
         @pl.when(jnp.logical_not(edge))
         def _():
@@ -138,6 +144,10 @@
         return 0
 
     lax.fori_loop(0, blocks, prefix, 0)
+
+    @pl.when(short)
+    def _():
+        attend(*learn(whole, slots // 2))
 
     doc = jnp.broadcast_to(doc_ref[...], (128, 128)).T
     at_s = lax.broadcasted_iota(jnp.int32, (128, 128), 1)
@@ -208,13 +218,19 @@
     state[:, :128] = stacked(halves(dkey[...] * slope), k)
     ds = jnp.concatenate(halves(dstate[...]), axis=0)
 
-    def pull(i, _):
-        k, v2, _ = loads(i)
+    def pull(i, size):
+        k, v2, _ = loads(i, size)
         dk = dot(ds, v2, NT)
-        state[:, :128] += stacked(halves((dk[:128] + dk[128:]) * sig[i]), k)
+        slope = sig[i, :, : size * 128]
+        state[:, :128] += stacked(halves((dk[:128] + dk[128:]) * slope), k)
         return 0
 
-    lax.fori_loop(0, blocks, pull, 0)
+    lax.fori_loop(0, blocks, lambda i, _: pull(i, slots), 0)
+
+    @pl.when(short)
+    def _():
+        pull(whole, slots // 2)
+
     gk = state[:64, :128] - state[64:, :128]
     pad = jnp.zeros((4, 128), F32)
     for j in range(heads):
@@ -435,6 +451,8 @@
     sq[...] = squares
     shares = [send(sq, sqin.at[k - 1], peers_h[k - 1]) for k in range(1, 4)]
     full[y, z, 0:64] = total[0:64].astype(jnp.bfloat16)
+    body, end = full.at[y, z, pl.ds(0, 64)], full.at[y, z, pl.ds(64, 16)]
+    parts = [send(body, body, peer) for peer in peers_z]
     for k, share in enumerate(shares):
         share.wait_recv()
         squares = squares + sqin[k]
@@ -443,8 +461,7 @@
     row = lax.broadcasted_iota(jnp.int32, (8, 128), 0)
     pair = jnp.where(row == 0, coarse, jnp.where(row == 1, squares - coarse, 0.0))
     full[y, z, 64:80] = jnp.concatenate([total[64:72], pair], axis=0).astype(jnp.bfloat16)
-    shard = full.at[y, z]
-    for part in [send(shard, shard, peer) for peer in peers_z]:
+    for part in parts + [send(end, end, peer) for peer in peers_z]:
         part.wait_recv()
     slab = full.at[y]
     both = [send(slab, slab, up), send(slab, slab, down)]
@@ -493,8 +510,8 @@
             pltpu.VMEM((8, 128), f32),
             pltpu.VMEM((3, 8, 128), f32),
             pltpu.VMEM((4, 8, 80, 128), jnp.bfloat16),
-            pltpu.SemaphoreType.DMA((32,)),
-            pltpu.SemaphoreType.DMA((32,)),
+            pltpu.SemaphoreType.DMA((40,)),
+            pltpu.SemaphoreType.DMA((40,)),
         ],
         compiler_params=pltpu.CompilerParams(collective_id=1, has_side_effects=True),
     )(g)

time: 178 us -> 176 us (0.989)
  no operation moved by 1% of the time
where the time goes in v2:
time: 176 us; the launch traced here: 177 us
  Pallas kernels  172 us (98%)
  local copies, waits for them, and re-layouts  3.65 us (2%)
    pallas_call x1, Pallas kernels, reduce(): pl.pallas_call(functools.partial(reduce_kernel, entries), out_shape=(jax....  71.1 us
    pallas_call x1, Pallas kernels, gather(): pl.pallas_call(gather_kernel, out_shape=jax.ShapeDtypeStruct((4, 8, 2) +...  60.7 us
    pallas_call x1, Pallas kernels, run(): pl.pallas_call(functools.partial(compute, span, tile, tokens), out_shape=...  39.8 us

profile of v2, /device:TPU:8, one launch (start us, length us, event | category | flops | bytes accessed | tf_op | source)
XLA Modules:
  0.0 176.9 jit_solution(5604240184730285972)
XLA Ops:
  0.6 1.0 maximum_bitcast_fusion
  1.6 0.7 copy.10
  2.3 60.7 %shard_map.93 = bf16[4,8,2,512,128]{4,3,2,1,0:T(8,128)(2,1)} custom-call(bf16[512,128]{1,0:T(8,128)(2,1)} %bitcast.15), custom_call_target="tpu_custom_call" | custom-call | tf_op jit(solution)/shard_map/pallas_call | solution.py:399
  63.1 39.8 %shard_map.94 = (bf16[128,32,128]{2,1,0:T(8,128)(2,1)}, f32[128,32,128]{2,1,0:T(8,128)}, f32[32,72,128]{2,1,0:T(8,128)}) custom-call(s32[128]{0:T(128)} %pos.1, s32[1,128]{1,0:T(1,128)} %bitcast.18, bf16[64,4,128,128]{3,2,1,0:T(8,128)(2,1)} %bitcast.10, bf16[64,4,128,128]{3,2,1,0:T(8,128)(2,1)} %bitcast.11, bf16[128,32,128]{2,1,0:T(8,128)(2,1)} %q_ref.1, ...), custom_call_target="tpu_custom_call" | custom-call | tf_op jit(solution)/shard_map/pallas_call | solution.py:244
  102.9 71.1 %shard_map.95 = (f32[32,64,128]{2,1,0:T(8,128)}, f32[2,64,128]{2,1,0:T(8,128)}) custom-call(f32[4,8,72,128]{3,2,1,0:T(8,128)} %bitcast.12), custom_call_target="tpu_custom_call" | custom-call | tf_op jit(solution)/shard_map/pallas_call | solution.py:494
  174.0 0.0 copy-start
  174.0 2.3 %copy.13 = f32[32,128,64]{1,2,0:T(8,128)} copy(f32[32,128,64]{1,2,0:T(8,128)} %bitcast.14) | data formatting | bytes 2097152
  176.3 0.0 copy-done
  176.3 0.6 copy.14
Async XLA Ops:
  174.0 2.4 %copy-start = (f32[2,64,128]{2,1,0:T(8,128)S(1)}, f32[2,64,128]{2,1,0:T(8,128)}, u32[]{:S(2)}) copy-start(f32[2,64,128]{2,1,0:T(8,128)} %get-tuple-element.13) | copy-start | bytes 196612
